TPU v7x, 256 devices: a whole 4x4x8 slice. The times are simulated.
256 devices in a mesh: gen: 8 (over z_lo, core), user: 16 (over x, y), cand: 2 (over z_hi).
Axes of the slice: x: 4, y: 4, z: 8 (z_hi: 2, z_lo: 4; z = z_hi * 4 + z_lo), core: 2. Of those that a mesh axis runs over, the one named last changes fastest.
Arguments:
- states: bfloat16 [16384, 4096], P(('user', 'cand')), may hold values from -6 to 6
- norm_gain: float32 [4096], replicated, may hold values from 0.1 to 1.9
- gate_weight: bfloat16 [4096, 7168], P('user', 'gen'), may hold values from -0.09375 to 0.09375
- up_weight: bfloat16 [4096, 7168], P('user', 'gen'), may hold values from -0.09375 to 0.09375
- down_weight: bfloat16 [7168, 4096], P('gen', 'user'), may hold values from -0.0625 to 0.0625
- proj_weight: bfloat16 [4096, 1024], P('gen'), may hold values from -0.09375 to 0.09375
- private_rows: bfloat16 [32768, 1024], P(('gen', 'user')), may hold values from -6 to 6
- enc_weight: bfloat16 [1024, 1024], replicated, may hold values from -0.1875 to 0.1875
- user_ids: int32 [32768], P(('gen', 'user')), may hold values from 0 to 31
Outputs:
- votes: float32 [16, 2, 128], P(None, 'cand')
Inputs may be any that keep to these rules, and one draw needn't show every extreme that they name: `user_ids`: a user is a pair of a block of 256 rows and a slot; no user has rows in two blocks.
All inputs are finite; a program needn't handle non-finite values.
Results may differ from a plain program's by a relative error of at most 0.0025.
Values may be sent and summed in bfloat16 or wider, within the bound.
No kernel may reach another device: no remote copies, remote signals or barrier semaphores. Data moves between devices by JAX's collectives and lax.ppermute only.
A program may use at most 128 MiB of HBM per device.

v0:
```python
import jax
import jax.numpy as jnp
from jax import lax
from jax.sharding import PartitionSpec as P

STEPS = 4
CAP = 8
USERS_DEV = 32


def unit_rows(matrix):
    return (matrix * lax.rsqrt(jnp.sum(matrix * matrix, axis=1, keepdims=True) + 1e-06)).astype(
        jnp.bfloat16
    )


def project_in(inputs, gate_part, up_part):

    def add_rows(piece):
        return jnp.dot(inputs, piece, preferred_element_type=jnp.float32)

    gate = add_rows(lax.all_gather(gate_part, "user", axis=0, tiled=True))
    up_proj = add_rows(lax.all_gather(up_part, "user", axis=0, tiled=True))
    return (gate, up_proj)


def shards(
    states,
    norm_gain,
    gate_weight,
    up_weight,
    down_weight,
    proj_weight,
    private_rows,
    enc_weight,
    user_ids,
):
    tok_rows, width_model = states.shape
    groups = tok_rows // STEPS
    values = states.astype(jnp.float32)
    normed = (
        values * lax.rsqrt(jnp.mean(values * values, axis=1, keepdims=True) + 1e-05) * norm_gain
    ).astype(jnp.bfloat16)
    gate_part, up_part, down_part = (gate_weight, up_weight, down_weight)
    gate, up_proj = project_in(normed, gate_part, up_part)
    hidden = (jax.nn.silu(gate) * up_proj).astype(jnp.bfloat16)
    mixed = jnp.dot(
        hidden,
        lax.all_gather(down_part, "user", axis=1, tiled=True),
        preferred_element_type=jnp.float32,
    )
    pooled_mlp = jnp.sum(mixed.reshape(-1, STEPS, width_model), axis=1)
    pooled_mlp = lax.psum_scatter(pooled_mlp, "gen", scatter_dimension=1, tiled=True)
    slab_width = pooled_mlp.shape[1]
    own_cols = lax.dynamic_slice_in_dim(values, lax.axis_index("gen") * slab_width, slab_width, 1)
    pooled_in = jnp.sum(own_cols.reshape(groups, STEPS, slab_width), axis=1)
    pooled = ((pooled_in + pooled_mlp) / STEPS).astype(jnp.bfloat16)
    partial_emb = jnp.dot(pooled, proj_weight, preferred_element_type=jnp.float32)
    embedding = lax.psum(partial_emb, "gen")
    candidate = unit_rows(embedding)
    every_cand = lax.all_gather(candidate, "user", axis=0, tiled=True)
    encoded = unit_rows(jnp.dot(private_rows, enc_weight, preferred_element_type=jnp.float32))
    scores = lax.dot_general(
        encoded, every_cand, (((1,), (1,)), ((), ())), preferred_element_type=jnp.float32
    )
    kernel = jnp.exp(scores * 60.0)
    totals = lax.psum(jnp.sum(kernel, axis=1), "cand")
    member = (user_ids[:, None] == jnp.arange(USERS_DEV, dtype=jnp.int32)[None, :]).astype(
        jnp.float32
    )
    counts = jnp.sum(member, axis=0)
    limit = jnp.minimum(1.0, CAP / jnp.maximum(counts, 1.0))
    row_cap = jnp.dot(member, limit, precision=lax.Precision.HIGHEST)
    row_total = private_rows.shape[0] * lax.axis_size("gen") * lax.axis_size("user")
    cand_total = every_cand.shape[0] * lax.axis_size("cand")
    weight_rows = row_cap / totals * (cand_total / row_total)
    partial_votes = jnp.dot(weight_rows, kernel, precision=lax.Precision.HIGHEST)
    votes = lax.psum(partial_votes, ("gen", "user"))
    return votes.reshape(lax.axis_size("user"), 1, groups)


def solution(mesh):
    return jax.shard_map(
        shards,
        mesh=mesh,
        in_specs=(
            P(("user", "cand"), None),
            P(),
            P("user", "gen"),
            P("user", "gen"),
            P("gen", "user"),
            P("gen", None),
            P(("gen", "user"), None),
            P(),
            P(("gen", "user")),
        ),
        out_specs=P(None, "cand", None),
        check_vma=False,
    )
```

profile of v0, /device:TPU:0, one launch (start us, length us, event | category | flops | bytes accessed | tf_op | source)
XLA Modules:
  0.0 810.1 jit_solution(10870717847516051505)
XLA Ops:
  6.5 0.0 copy-start
  6.5 0.0 copy-start.1
  6.5 0.0 all-gather.5.cloned.1.call-start
  6.5 0.7 all-gather.5.cloned.1.call-update
  7.3 0.0 all-gather.7.cloned.1.call-start
  7.3 0.7 all-gather.7.cloned.1.call-update
  8.0 0.0 all-gather.9.cloned.1.call-start
  8.1 0.7 all-gather.9.cloned.1.call-update
  8.7 0.0 reduce-scatter.2.cloned.1.call-start
  8.8 3.1 multiply_reduce_fusion
  11.9 70.3 %all-gather.5.cloned.1.call-done = bf16[4096,896]{1,0:T(8,128)(2,1)} async-done(((bf16[256,896]{1,0:T(8,128)(2,1)}), bf16[4096,896]{1,0:T(8,128)(2,1)}) %all-gather.5.cloned.1.call-update) | async-done | bytes 7340048 | tf_op jit(solution)/shard_map/all_gather | solution.py:22
  82.2 0.0 copy-done.1
  82.2 10.1 %fusion.1 = f32[512,896]{1,0:T(8,128)} fusion(bf16[4096,896]{1,0:T(8,128)(2,1)} %all-gather.5.cloned.1.call-done, f32[4096]{0:T(1024)S(1)} %copy-done.1, f32[512]{0:T(512)S(1)} %add_rsqrt_fusion, bf16[512,4096]{1,0:T(8,128)(2,1)} %param.9), kind=kOutput, calls=%fused_computation.5 | convolution fusion | flops 3766484992 | bytes 13387776 | tf_op jit(solution)/shard_map/dot_general | solution.py:20
  92.3 63.2 %all-gather.7.cloned.1.call-done = bf16[4096,896]{1,0:T(8,128)(2,1)} async-done(((bf16[256,896]{1,0:T(8,128)(2,1)}), bf16[4096,896]{1,0:T(8,128)(2,1)}) %all-gather.7.cloned.1.call-update) | async-done | bytes 7340048 | tf_op jit(solution)/shard_map/all_gather | solution.py:23
  155.6 79.3 %all-gather.9.cloned.1.call-done = bf16[896,4096]{1,0:T(8,128)(2,1)} async-done(((bf16[896,256]{1,0:T(8,128)(2,1)}), bf16[896,4096]{1,0:T(8,128)(2,1)}) %all-gather.9.cloned.1.call-update) | async-done | bytes 7340048 | tf_op jit(solution)/shard_map/all_gather | solution.py:49
  234.8 17.4 %fusion.2 = f32[512,4096]{1,0:T(8,128)} fusion(bf16[896,4096]{1,0:T(8,128)(2,1)} %all-gather.9.cloned.1.call-done, f32[512,896]{1,0:T(8,128)} %fusion.1, bf16[4096,896]{1,0:T(8,128)(2,1)} %all-gather.7.cloned.1.call-done, f32[4096]{0:T(1024)S(1)} %copy-done.1, f32[512]{0:T(512)S(1)} %add_rsqrt_fusion, bf16[512,4096]{1,0:T(8,128)(2,1)} %param.9), kind=kOutput, calls=%fused_computation.9 | convolution fusion | flops 7527333888 | bytes 29116416 | tf_op jit(solution)/shard_map/dot_general | solution.py:47
  252.2 9.8 %reshape.32 = f32[128,4,4096]{2,1,0:T(4,128)} reshape(f32[512,4096]{1,0:T(8,128)} %fusion.2) | data formatting | bytes 16777216 | tf_op jit(solution)/shard_map/reshape | solution.py:52
  262.0 10.0 %reduce_sum.67 = f32[128,4096]{1,0:T(8,128)} reduce(f32[128,4,4096]{2,1,0:T(4,128)} %reshape.32, f32[]{:T(128)} %constant.15.clone.1), dimensions={1}, to_apply=%region_4.5 | reduce | flops 1572864 | bytes 10485764 | tf_op jit(solution)/shard_map/reduce_sum | solution.py:52
  272.0 0.0 reduce-scatter.2.cloned.1.call-update
  272.1 0.0 all-reduce.2.cloned.1.call-start
  272.1 6.5 convert_element_type.23
  278.6 1.3 constant_dynamic-slice_fusion
  279.9 0.0 copy-start.2
  279.9 1.3 reshape.31
  281.2 1.8 reduce_sum.65
  283.1 29.9 %reduce-scatter.2.cloned.1.call-done = f32[128,512]{1,0:T(8,128)} async-done(((f32[128,4096]{1,0:T(8,128)}), f32[128,512]{1,0:T(8,128)}) %reduce-scatter.2.cloned.1.call-update) | async-done | bytes 262160 | tf_op jit(solution)/shard_map/reduce_scatter | solution.py:53
  313.0 2.4 fusion.4
  315.4 0.0 all-reduce.2.cloned.1.call-update
  315.4 0.3 all-gather.11.cloned.1.call-start
  315.7 70.7 %all-reduce.2.cloned.1.call-done = f32[128,1024]{1,0:T(8,128)} async-done(((f32[128,1024]{1,0:T(8,128)}), f32[128,1024]{1,0:T(8,128)}) %all-reduce.2.cloned.1.call-update) | async-done | bytes 524304 | tf_op jit(solution)/shard_map/psum | solution.py:59
  386.3 1.2 multiply_reduce_fusion.2
  387.5 1.8 multiply_convert_fusion.8
  389.3 0.0 all-gather.11.cloned.1.call-update
  389.4 0.0 copy-done.2
  389.4 0.1 convert_reduce_fusion
  389.5 0.0 copy-done
  389.5 1.8 multiply_reduce_fusion.1
  391.3 0.1 fusion.6
  391.5 53.5 %all-gather.11.cloned.1.call-done = bf16[2048,1024]{1,0:T(8,128)(2,1)} async-done(((bf16[128,1024]{1,0:T(8,128)(2,1)}), bf16[2048,1024]{1,0:T(8,128)(2,1)}) %all-gather.11.cloned.1.call-update) | async-done | bytes 4194320 | tf_op jit(solution)/shard_map/all_gather | solution.py:61
  445.0 4.9 fusion.16
  449.8 8.8 %psum.22 = f32[256]{0:T(256)S(1)} all-reduce(f32[256]{0:T(256)S(1)} %get-tuple-element.7), channel_id=1, replica_groups=mesh['gen'=8,'user'=16,'cand'=2] {'cand'}, use_global_device_ids=true, to_apply=%region_9.10 | all-reduce | flops 256 | bytes 2048 | tf_op jit(solution)/shard_map/psum | solution.py:67
  458.6 2.7 convolution_bitcast_fusion
  461.3 341.9 %psum.23 = f32[16,1,128]{2,1,0:T(1,128)} all-reduce(f32[16,1,128]{2,1,0:T(1,128)S(1)} %convolution_bitcast_fusion), channel_id=1, replica_groups=mesh['gen'=8,'user'=16,'cand'=2] {'gen','user'}, use_global_device_ids=true, to_apply=%region_10.11 | all-reduce | flops 2048 | bytes 16384 | tf_op jit(solution)/shard_map/psum | solution.py:78
  (4 shorter events, 0.0 us)
Async XLA Ops:
  6.5 383.0 %copy-start = (bf16[1024,1024]{1,0:T(8,128)(2,1)S(1)}, bf16[1024,1024]{1,0:T(8,128)(2,1)}, u32[]{:S(2)}) copy-start(bf16[1024,1024]{1,0:T(8,128)(2,1)} %param.16) | copy-start | bytes 6291460
  6.5 75.7 %copy-start.1 = (f32[4096]{0:T(1024)S(1)}, f32[4096]{0:T(1024)}, u32[]{:S(2)}) copy-start(f32[4096]{0:T(1024)} %param.10) | copy-start | bytes 49156
  6.5 75.7 %all-gather.5.cloned.1.call-start = ((), (), s32[]{:S(2)}) async-start(), calls=%async_computation.1 | async-start | bytes 7798784 | tf_op jit(solution)/shard_map/all_gather | solution.py:22
  7.3 148.3 %all-gather.7.cloned.1.call-start = ((), (), s32[]{:S(2)}) async-start(), calls=%async_computation.2 | async-start | bytes 7798784 | tf_op jit(solution)/shard_map/all_gather | solution.py:23
  8.0 226.8 %all-gather.9.cloned.1.call-start = ((), (), s32[]{:S(2)}) async-start(), calls=%async_computation.3 | async-start | bytes 7798784 | tf_op jit(solution)/shard_map/all_gather | solution.py:49
  8.7 304.2 %reduce-scatter.2.cloned.1.call-start = ((), (), s32[]{:S(2)}) async-start(), calls=%async_computation.4 | async-start | bytes 2359296 | tf_op jit(solution)/shard_map/reduce_scatter | solution.py:53
  272.1 114.3 %all-reduce.2.cloned.1.call-start = ((), (), s32[]{:S(2)}) async-start(), calls=%async_computation.5 | async-start | bytes 1048576 | tf_op jit(solution)/shard_map/psum | solution.py:59
  279.9 109.5 %copy-start.2 = (s32[256]{0:T(256)S(1)}, s32[256]{0:T(256)}, u32[]{:S(2)}) copy-start(s32[256]{0:T(256)} %param.17) | copy-start | bytes 3076
  315.4 129.5 %all-gather.11.cloned.1.call-start = ((), (), s32[]{:S(2)}) async-start(), calls=%async_computation.6 | async-start | bytes 4456448 | tf_op jit(solution)/shard_map/all_gather | solution.py:61
Sparse Core Ops, SparseCore 0:
  9.8 72.3 all-gather.4
  84.7 70.8 all-gather.6
  158.0 76.7 all-gather.8
  272.2 40.7 reduce-scatter.1
  315.5 70.7 all-reduce.1
  389.5 55.4 all-gather.10
where the time goes:
time: 811 us; the launch traced here: 810 us
  waiting for transfers between devices  369 us (45%)
  blocking collectives  351 us (43%)
  matrix products  39.5 us (5%)
  other arithmetic  24.6 us (3%)
  between operations  13.5 us (2%)
  local copies, waits for them, and re-layouts  12.4 us (2%)
    psum x1, blocking collectives, shards(): votes = lax.psum(partial_votes, ('gen', 'user'))  342 us
    all_gather x1, waiting for transfers between devices, shards(): lax.all_gather(down_part, 'user', axis=1, tiled=True)  79.3 us
    psum x1, waiting for transfers between devices, shards(): embedding = lax.psum(partial_emb, 'gen')  70.7 us
    all_gather x1, waiting for transfers between devices, project_in(): gate = add_rows(lax.all_gather(gate_part, 'user', axis=0, tiled=True))  70.3 us
    all_gather x1, waiting for transfers between devices, project_in(): up_proj = add_rows(lax.all_gather(up_part, 'user', axis=0, tiled=True))  63.2 us
    all_gather x1, waiting for transfers between devices, shards(): every_cand = lax.all_gather(candidate, 'user', axis=0, tiled=True)  53.5 us
    reduce_scatter x1, waiting for transfers between devices, shards(): lax.psum_scatter(pooled_mlp, 'gen', scatter_dimension=1, tiled=True)  29.9 us
    dot_general x1, matrix products, shards(): jnp.dot(hidden, lax.all_gather(down_part, 'user', axis=1, tiled=True), pr...  17.4 us
  transfers between devices with their start and end apart: 6, of which 6 were waited for; matrix products, arithmetic and copies ran while one was open for 3% of the time, Pallas kernels for 0%

commit v1 on v0

--- a/solution.py
+++ b/solution.py
@@ -75,7 +75,7 @@
     cand_total = every_cand.shape[0] * lax.axis_size("cand")
     weight_rows = row_cap / totals * (cand_total / row_total)
     partial_votes = jnp.dot(weight_rows, kernel, precision=lax.Precision.HIGHEST)
-    votes = lax.psum(partial_votes, ("gen", "user"))
+    votes = lax.psum(lax.psum(partial_votes, "user"), "gen")
     return votes.reshape(lax.axis_size("user"), 1, groups)
 
 

time: 811 us -> 525 us (0.65)
  blocking collectives: 351 us -> 62.2 us
    psum x1 -> x2, blocking collectives: 342 us -> 53.3 us  [shards(): votes = lax.psum(lax.psum(partial_votes, 'user'), 'gen')]
  transfers between devices with their start and end apart: 6 -> 6, of which waited for: 6 -> 6; matrix products, arithmetic and copies ran while one was open for 3% -> 5% of each run, Pallas kernels for 0% -> 0%
where the time goes in v1:
time: 525 us; the launch traced here: 522 us
  waiting for transfers between devices  369 us (70%)
  blocking collectives  62.2 us (12%)
  matrix products  39.5 us (8%)
  other arithmetic  24.6 us (5%)
  between operations  13.5 us (3%)
  local copies, waits for them, and re-layouts  12.4 us (2%)
    all_gather x1, waiting for transfers between devices, shards(): lax.all_gather(down_part, 'user', axis=1, tiled=True)  79.3 us
    psum x1, waiting for transfers between devices, shards(): embedding = lax.psum(partial_emb, 'gen')  70.7 us
    all_gather x1, waiting for transfers between devices, project_in(): gate = add_rows(lax.all_gather(gate_part, 'user', axis=0, tiled=True))  70.3 us
    all_gather x1, waiting for transfers between devices, project_in(): up_proj = add_rows(lax.all_gather(up_part, 'user', axis=0, tiled=True))  63.2 us
    all_gather x1, waiting for transfers between devices, shards(): every_cand = lax.all_gather(candidate, 'user', axis=0, tiled=True)  53.5 us
    psum x2, blocking collectives, shards(): votes = lax.psum(lax.psum(partial_votes, 'user'), 'gen')  53.3 us
    reduce_scatter x1, waiting for transfers between devices, shards(): lax.psum_scatter(pooled_mlp, 'gen', scatter_dimension=1, tiled=True)  29.9 us
    dot_general x1, matrix products, shards(): jnp.dot(hidden, lax.all_gather(down_part, 'user', axis=1, tiled=True), pr...  17.4 us
  transfers between devices with their start and end apart: 6, of which 6 were waited for; matrix products, arithmetic and copies ran while one was open for 5% of the time, Pallas kernels for 0%

profile of v1, /device:TPU:0, one launch (start us, length us, event | category | flops | bytes accessed | tf_op | source)
XLA Modules:
  0.0 521.5 jit_solution(14013411171418830363)
XLA Ops:
  6.5 0.0 copy-start
  6.5 0.0 copy-start.1
  6.5 0.0 all-gather.5.cloned.1.call-start
  6.5 0.7 all-gather.5.cloned.1.call-update
  7.3 0.0 all-gather.7.cloned.1.call-start
  7.3 0.7 all-gather.7.cloned.1.call-update
  8.0 0.0 all-gather.9.cloned.1.call-start
  8.1 0.7 all-gather.9.cloned.1.call-update
  8.7 0.0 reduce-scatter.2.cloned.1.call-start
  8.8 3.1 multiply_reduce_fusion
  11.9 70.3 %all-gather.5.cloned.1.call-done = bf16[4096,896]{1,0:T(8,128)(2,1)} async-done(((bf16[256,896]{1,0:T(8,128)(2,1)}), bf16[4096,896]{1,0:T(8,128)(2,1)}) %all-gather.5.cloned.1.call-update) | async-done | bytes 7340048 | tf_op jit(solution)/shard_map/all_gather | solution.py:22
  82.2 0.0 copy-done.1
  82.2 10.1 %fusion.1 = f32[512,896]{1,0:T(8,128)} fusion(bf16[4096,896]{1,0:T(8,128)(2,1)} %all-gather.5.cloned.1.call-done, f32[4096]{0:T(1024)S(1)} %copy-done.1, f32[512]{0:T(512)S(1)} %add_rsqrt_fusion, bf16[512,4096]{1,0:T(8,128)(2,1)} %param.9), kind=kOutput, calls=%fused_computation.5 | convolution fusion | flops 3766484992 | bytes 13387776 | tf_op jit(solution)/shard_map/dot_general | solution.py:20
  92.3 63.2 %all-gather.7.cloned.1.call-done = bf16[4096,896]{1,0:T(8,128)(2,1)} async-done(((bf16[256,896]{1,0:T(8,128)(2,1)}), bf16[4096,896]{1,0:T(8,128)(2,1)}) %all-gather.7.cloned.1.call-update) | async-done | bytes 7340048 | tf_op jit(solution)/shard_map/all_gather | solution.py:23
  155.6 79.3 %all-gather.9.cloned.1.call-done = bf16[896,4096]{1,0:T(8,128)(2,1)} async-done(((bf16[896,256]{1,0:T(8,128)(2,1)}), bf16[896,4096]{1,0:T(8,128)(2,1)}) %all-gather.9.cloned.1.call-update) | async-done | bytes 7340048 | tf_op jit(solution)/shard_map/all_gather | solution.py:49
  234.8 17.4 %fusion.2 = f32[512,4096]{1,0:T(8,128)} fusion(bf16[896,4096]{1,0:T(8,128)(2,1)} %all-gather.9.cloned.1.call-done, f32[512,896]{1,0:T(8,128)} %fusion.1, bf16[4096,896]{1,0:T(8,128)(2,1)} %all-gather.7.cloned.1.call-done, f32[4096]{0:T(1024)S(1)} %copy-done.1, f32[512]{0:T(512)S(1)} %add_rsqrt_fusion, bf16[512,4096]{1,0:T(8,128)(2,1)} %param.9), kind=kOutput, calls=%fused_computation.8 | convolution fusion | flops 7527333888 | bytes 29116416 | tf_op jit(solution)/shard_map/dot_general | solution.py:47
  252.2 9.8 %reshape.32 = f32[128,4,4096]{2,1,0:T(4,128)} reshape(f32[512,4096]{1,0:T(8,128)} %fusion.2) | data formatting | bytes 16777216 | tf_op jit(solution)/shard_map/reshape | solution.py:52
  262.0 10.0 %reduce_sum.67 = f32[128,4096]{1,0:T(8,128)} reduce(f32[128,4,4096]{2,1,0:T(4,128)} %reshape.32, f32[]{:T(128)} %constant.15.clone.1), dimensions={1}, to_apply=%region_4.5 | reduce | flops 1572864 | bytes 10485764 | tf_op jit(solution)/shard_map/reduce_sum | solution.py:52
  272.0 0.0 reduce-scatter.2.cloned.1.call-update
  272.1 0.0 all-reduce.2.cloned.1.call-start
  272.1 6.5 %convert_element_type.23 = f32[512,4096]{1,0:T(8,128)} convert(bf16[512,4096]{1,0:T(8,128)(2,1)} %param.9) | non-fusion elementwise | flops 2097152 | bytes 12582912 | tf_op jit(solution)/shard_map/convert_element_type | solution.py:40
  278.6 1.3 constant_dynamic-slice_fusion
  279.9 0.0 copy-start.2
  279.9 1.3 reshape.31
  281.2 1.8 reduce_sum.65
  283.1 29.9 %reduce-scatter.2.cloned.1.call-done = f32[128,512]{1,0:T(8,128)} async-done(((f32[128,4096]{1,0:T(8,128)}), f32[128,512]{1,0:T(8,128)}) %reduce-scatter.2.cloned.1.call-update) | async-done | bytes 262160 | tf_op jit(solution)/shard_map/reduce_scatter | solution.py:53
  313.0 2.4 fusion.4
  315.4 0.0 all-reduce.2.cloned.1.call-update
  315.4 0.3 all-gather.11.cloned.1.call-start
  315.7 70.7 %all-reduce.2.cloned.1.call-done = f32[128,1024]{1,0:T(8,128)} async-done(((f32[128,1024]{1,0:T(8,128)}), f32[128,1024]{1,0:T(8,128)}) %all-reduce.2.cloned.1.call-update) | async-done | bytes 524304 | tf_op jit(solution)/shard_map/psum | solution.py:59
  386.3 1.2 multiply_reduce_fusion.2
  387.5 1.8 multiply_convert_fusion.8
  389.3 0.0 all-gather.11.cloned.1.call-update
  389.4 0.0 copy-done.2
  389.4 0.1 convert_reduce_fusion
  389.5 0.0 copy-done
  389.5 1.8 multiply_reduce_fusion.1
  391.3 0.1 fusion.6
  391.5 53.5 %all-gather.11.cloned.1.call-done = bf16[2048,1024]{1,0:T(8,128)(2,1)} async-done(((bf16[128,1024]{1,0:T(8,128)(2,1)}), bf16[2048,1024]{1,0:T(8,128)(2,1)}) %all-gather.11.cloned.1.call-update) | async-done | bytes 4194320 | tf_op jit(solution)/shard_map/all_gather | solution.py:61
  445.0 4.9 fusion.16
  449.8 8.8 %psum.29 = f32[256]{0:T(256)S(1)} all-reduce(f32[256]{0:T(256)S(1)} %get-tuple-element.7), channel_id=1, replica_groups=mesh['gen'=8,'user'=16,'cand'=2] {'cand'}, use_global_device_ids=true, to_apply=%region_9.10 | all-reduce | flops 256 | bytes 2048 | tf_op jit(solution)/shard_map/psum | solution.py:67
  458.6 2.7 fusion.17
  461.3 38.9 %psum.30 = f32[2048]{0:T(1024)S(1)} all-reduce(f32[2048]{0:T(1024)S(1)} %bitcast.16), channel_id=1, replica_groups=mesh['gen'=8,'user'=16,'cand'=2] {'user'}, use_global_device_ids=true, to_apply=%region_10.11 | all-reduce | flops 2048 | bytes 16384 | tf_op jit(solution)/shard_map/psum | solution.py:78
  500.3 14.4 %psum.31 = f32[16,1,128]{2,1,0:T(1,128)} all-reduce(f32[16,1,128]{2,1,0:T(1,128)S(1)} %bitcast.17), channel_id=1, replica_groups=mesh['gen'=8,'user'=16,'cand'=2] {'gen'}, use_global_device_ids=true, to_apply=%region_11.12 | all-reduce | flops 2048 | bytes 16384 | tf_op jit(solution)/shard_map/psum | solution.py:78
  (4 shorter events, 0.0 us)
Async XLA Ops:
  6.5 383.0 %copy-start = (bf16[1024,1024]{1,0:T(8,128)(2,1)S(1)}, bf16[1024,1024]{1,0:T(8,128)(2,1)}, u32[]{:S(2)}) copy-start(bf16[1024,1024]{1,0:T(8,128)(2,1)} %param.16) | copy-start | bytes 6291460
  6.5 75.7 %copy-start.1 = (f32[4096]{0:T(1024)S(1)}, f32[4096]{0:T(1024)}, u32[]{:S(2)}) copy-start(f32[4096]{0:T(1024)} %param.10) | copy-start | bytes 49156
  6.5 75.7 %all-gather.5.cloned.1.call-start = ((), (), s32[]{:S(2)}) async-start(), calls=%async_computation.1 | async-start | bytes 7798784 | tf_op jit(solution)/shard_map/all_gather | solution.py:22
  7.3 148.3 %all-gather.7.cloned.1.call-start = ((), (), s32[]{:S(2)}) async-start(), calls=%async_computation.2 | async-start | bytes 7798784 | tf_op jit(solution)/shard_map/all_gather | solution.py:23
  8.0 226.8 %all-gather.9.cloned.1.call-start = ((), (), s32[]{:S(2)}) async-start(), calls=%async_computation.3 | async-start | bytes 7798784 | tf_op jit(solution)/shard_map/all_gather | solution.py:49
  8.7 304.2 %reduce-scatter.2.cloned.1.call-start = ((), (), s32[]{:S(2)}) async-start(), calls=%async_computation.4 | async-start | bytes 2359296 | tf_op jit(solution)/shard_map/reduce_scatter | solution.py:53
  272.1 114.3 %all-reduce.2.cloned.1.call-start = ((), (), s32[]{:S(2)}) async-start(), calls=%async_computation.5 | async-start | bytes 1048576 | tf_op jit(solution)/shard_map/psum | solution.py:59
  279.9 109.5 %copy-start.2 = (s32[256]{0:T(256)S(1)}, s32[256]{0:T(256)}, u32[]{:S(2)}) copy-start(s32[256]{0:T(256)} %param.17) | copy-start | bytes 3076
  315.4 129.5 %all-gather.11.cloned.1.call-start = ((), (), s32[]{:S(2)}) async-start(), calls=%async_computation.6 | async-start | bytes 4456448 | tf_op jit(solution)/shard_map/all_gather | solution.py:61
Sparse Core Ops, SparseCore 0:
  9.8 72.3 all-gather.4
  84.7 70.8 all-gather.6
  158.0 76.7 all-gather.8
  272.2 40.7 reduce-scatter.1
  315.5 70.7 all-reduce.1
  389.5 55.4 all-gather.10
